TPU v7x, 32 devices: a whole 2x2x4 slice. The times are simulated.
32 devices in a mesh: grp: 4 (over z), mem: 8 (over y, x, core).
Axes of the slice: x: 2, y: 2, z: 4, core: 2. Of those that a mesh axis runs over, the one named last changes fastest.
Arguments:
- child_means: float32 [65536, 64], P(('grp', 'mem')), may hold values from -48 to 48
- child_variances: float32 [65536, 64], P(('grp', 'mem')), may hold values from 0.2 to 2
- virtual_counts: int32 [65536], P(('grp', 'mem')), may hold values from 1 to 4
- assignment: int32 [65536, 1], P(('grp', 'mem')), may hold values from 0 to 511
Outputs:
- parent_means: float32 [512, 64], P('mem')
- parent_variances: float32 [512, 64], P('mem')
- parent_weights: float32 [512], P('mem')
All inputs are finite; a program needn't handle non-finite values.
Results may differ from a plain program's by a relative error of at most 0.0003.
Values sent between devices are 32-bit elements; how exact they have to be, the bound alone decides.
A program may use at most 64 MiB of HBM per device.

v0:
```python
import math

import jax
import jax.numpy as jnp
from jax import lax
from jax.sharding import PartitionSpec as P

P_SIZE = 512
ITERS = 2


def child_features(means, variances):
    return jnp.concatenate([means, variances + means * means], axis=1)


def accumulate(features, extras, weigh):
    row_count = features.shape[0]
    block = math.gcd(row_count, 1024)
    turns = row_count // block
    pieces = (features.reshape(turns, block, features.shape[1]),) + tuple(
        (extra.reshape((turns, block) + extra.shape[1:]) for extra in extras)
    )

    def advance(carry, piece):
        weights = weigh(*piece)
        sums = carry[0] + lax.dot_general(
            weights,
            piece[0],
            (((0,), (0,)), ((), ())),
            precision=lax.Precision.HIGHEST,
            preferred_element_type=jnp.float32,
        )
        counts = carry[1] + jnp.sum(weights, axis=0)
        return ((sums, counts), None)

    start_sums = (
        jnp.zeros((P_SIZE, features.shape[1]), jnp.float32),
        jnp.zeros((P_SIZE,), jnp.float32),
    )
    return lax.scan(advance, start_sums, pieces)[0]


def maximize(counts, sums, total):
    width = sums.shape[1] // 2
    mass = counts + 1.0
    means = sums[:, :width] / mass[:, None]
    second = (sums[:, width:] + 1.0) / mass[:, None]
    return (means, second - means * means, mass / (total + P_SIZE))


def parent_table(means, variances, weights):
    inverse = 1.0 / variances
    table = jnp.concatenate([-2.0 * means * inverse, inverse], axis=1)
    offset = jnp.sum(jnp.log(2.0 * math.pi * variances) + means * means * inverse, axis=1)
    return (table, offset, jnp.log(weights))


def soft_weights(block_features, block_virtual, table, offset, log_weight):
    width = block_features.shape[1] // 2
    cross = lax.dot_general(
        block_features,
        table,
        (((1,), (1,)), ((), ())),
        precision=lax.Precision.HIGHEST,
        preferred_element_type=jnp.float32,
    )
    ell = -0.5 / width * (cross + offset[None, :])
    score = log_weight[None, :] + block_virtual[:, None] * ell
    top = jnp.max(score, axis=1, keepdims=True)
    expd = jnp.exp(score - top)
    resp = expd / jnp.sum(expd, axis=1, keepdims=True)
    return resp * block_virtual[:, None]


def shards(child_means, child_variances, virtual_counts, assignment):
    features = child_features(child_means, child_variances)
    virtual = virtual_counts.astype(jnp.float32)
    labels = jnp.arange(P_SIZE, dtype=jnp.int32)

    def initial_weights(block_features, block_virtual, block_assign):
        return (block_assign == labels[None, :]).astype(jnp.float32) * block_virtual[:, None]

    sums, counts = accumulate(features, (virtual, assignment), initial_weights)
    total = lax.psum(jnp.sum(virtual), ("grp", "mem"))

    def combine(local_sums, local_counts):
        shared = (
            lax.psum_scatter(local_sums, "mem", scatter_dimension=0, tiled=True),
            lax.psum_scatter(local_counts, "mem", scatter_dimension=0, tiled=True),
        )
        return lax.psum((shared[0], shared[1]), "grp")

    own_sums, own_counts = combine(sums, counts)
    means, variances, weights = maximize(own_counts, own_sums, total)
    for iteration in range(ITERS):
        all_means, all_variances, all_weights = (
            lax.all_gather(means, "mem", axis=0, tiled=True),
            lax.all_gather(variances, "mem", axis=0, tiled=True),
            lax.all_gather(weights, "mem", axis=0, tiled=True),
        )
        table, offset, log_weight = parent_table(all_means, all_variances, all_weights)

        def weigh(block_features, block_virtual):
            return soft_weights(block_features, block_virtual, table, offset, log_weight)

        sums, counts = accumulate(features, (virtual,), weigh)
        own_sums, own_counts = combine(sums, counts)
        means, variances, weights = maximize(own_counts, own_sums, total)
    return (means, variances, weights)


def solution(mesh):
    in_specs = (
        P(("grp", "mem"), None),
        P(("grp", "mem"), None),
        P(("grp", "mem")),
        P(("grp", "mem"), None),
    )
    out_specs = (P("mem", None), P("mem", None), P("mem"))
    return jax.shard_map(shards, mesh=mesh, in_specs=in_specs, out_specs=out_specs, check_vma=False)
```

profile of v0, /device:TPU:0, one launch (start us, length us, event | category | flops | bytes accessed | tf_op | source)
XLA Modules:
  0.0 293.5 jit_solution(11252077472539837460)
XLA Ops:
  10.1 8.4 %while.39 = (s32[]{:T(128)}, f32[512,128]{1,0:T(8,128)S(1)}, f32[512]{0:T(512)S(1)}, s32[2,1024,1]{1,2,0:T(1,128)S(1)}, f32[2,1024]{1,0:T(2,128)S(1)}, /*index=5*/f32[2,1024,128]{2,1,0:T(8,128)S(1)}, s32[]{:T(128)}, s32[]{:T(128)}) while((s32[]{:T(128)}, f32[512,128]{1,0:T(8,128)S(1)}, f32[512]{0:T(512)S(1)}, ...), condition=%wide.region_2.3_spmd.clone, body=%wide.region_0.2_spmd.clone.sunk | while | flops 808059392 | bytes 1089644 | solution.py:40
  10.1 3.8 %fusion.56 = f32[512,128]{1,0:T(8,128)S(1)} fusion(f32[1024]{0:T(1024)S(1)} %bitcast.56, s32[1024]{0:T(1024)S(1)} %bitcast.58, f32[2,1024,128]{2,1,0:T(8,128)S(1)} %get-tuple-element.448, s32[]{:T(128)} %get-tuple-element.435, f32[512,128]{1,0:T(8,128)S(1)} %get-tuple-element.436, pred[]{:T(512)S(6)} %compare.9), kind=kOutput, calls=%fused_computation.5.clone.1 | convolution fusion | flops 806486016 | bytes 1056773 | tf_op jit(solution)/shard_map/while/body/eval_jaxpr/dot_general | solution.py:26
  14.3 3.8 %fusion.56 = f32[512,128]{1,0:T(8,128)S(1)} fusion(f32[1024]{0:T(1024)S(1)} %bitcast.56, s32[1024]{0:T(1024)S(1)} %bitcast.58, f32[2,1024,128]{2,1,0:T(8,128)S(1)} %get-tuple-element.448, s32[]{:T(128)} %get-tuple-element.435, f32[512,128]{1,0:T(8,128)S(1)} %get-tuple-element.436, pred[]{:T(512)S(6)} %compare.9), kind=kOutput, calls=%fused_computation.5.clone.1 | convolution fusion | flops 806486016 | bytes 1056773 | tf_op jit(solution)/shard_map/while/body/eval_jaxpr/dot_general | solution.py:26
  19.8 42.2 %psum.50 = f32[]{:T(128)} all-reduce(f32[]{:T(128)} %convert_reduce_fusion), channel_id=1, replica_groups=mesh['grp'=4,'mem'=8] {'grp','mem'}, use_global_device_ids=true, to_apply=%region_9.10 | all-reduce | flops 1 | bytes 8 | tf_op jit(solution)/shard_map/psum | solution.py:84
  63.2 13.0 %all-reduce.2 = f32[512]{0:T(512)S(1)} all-reduce(f32[512]{0:T(512)S(1)} %get-tuple-element.127), channel_id=2, replica_groups=mesh['grp'=4,'mem'=8] {'mem'}, use_global_device_ids=true, to_apply=%region_5.6.clone | all-reduce | flops 512 | bytes 4096
  77.6 18.8 %all-reduce.7 = (f32[64]{0:T(128)S(1)}, f32[64,128]{1,0:T(8,128)S(1)}) all-reduce(f32[64]{0:T(128)S(1)} %dynamic-slice.3, f32[64,128]{1,0:T(8,128)} %reduce-scatter.4.cloned.1.call-done), channel_id=1, replica_groups=mesh['grp'=4,'mem'=8] {'grp'}, use_global_device_ids=true, to_apply=%region_6.7 | all-reduce | flops 8256 | bytes 66048 | tf_op jit(solution)/shard_map/psum | solution.py:91
  96.6 9.1 %all_gather.19 = f32[512,64]{1,0:T(8,128)S(1)} all-gather(f32[64,64]{1,0:T(8,128)S(1)} %get-tuple-element.274), channel_id=1, replica_groups=mesh['grp'=4,'mem'=8] {'mem'}, dimensions={0}, use_global_device_ids=true | all-gather | bytes 147456 | tf_op jit(solution)/shard_map/all_gather | solution.py:97
  105.7 8.5 %all_gather.20 = f32[512,64]{1,0:T(8,128)S(1)} all-gather(f32[64,64]{1,0:T(8,128)S(1)} %get-tuple-element.275), channel_id=1, replica_groups=mesh['grp'=4,'mem'=8] {'mem'}, dimensions={0}, use_global_device_ids=true | all-gather | bytes 147456 | tf_op jit(solution)/shard_map/all_gather | solution.py:98
  114.2 13.4 %all-reduce = f32[512]{0:T(512)S(1)} all-reduce(f32[512]{0:T(512)S(1)} %get-tuple-element.281), channel_id=1, replica_groups=mesh['grp'=4,'mem'=8] {'mem'}, use_global_device_ids=true, to_apply=%add | all-reduce | flops 512 | bytes 4096
  127.9 12.2 %while.40 = (s32[]{:T(128)}, f32[512,128]{1,0:T(8,128)}, f32[512]{0:T(512)S(1)}, f32[512]{0:T(512)S(1)}, f32[2,1024,128]{2,1,0:T(8,128)S(1)}, /*index=5*/f32[512...) while((s32[]{:T(128)}, f32[512,128]{1,0:T(8,128)}, ...), condition=%wide.region_14.15_spmd.clone, body=%wide.region_10.14_spmd.clone.sunk | while | flops 1617559040 | bytes 10293372 | solution.py:40
  130.8 2.7 convolution_add_fusion.4
  136.5 3.7 %convolution_add_fusion.4 = f32[512,128]{1,0:T(8,128)} fusion(f32[2,1024,128]{2,1,0:T(8,128)S(1)} %get-tuple-element.475, s32[]{:T(128)} %get-tuple-element.461, f32[1024,512]{0,1:T(8,128)S(1)} %get-tuple-element.415, f32[1024]{0:T(1024)S(1)} %bitcast.52, f32[1024]{0:T(1024)S(1)} %fusion.60, f32[1024]{0:T(1024)S(1)} %get-tuple-element.416, ...), kind=kOutput, calls=%fused_computation.20.clone.1 | convolution fusion | flops 807010304 | bytes 3158021 | tf_op jit(solution)/shard_map/while/body/eval_jaxpr/dot_general | solution.py:26
  140.2 11.8 %all-reduce.3 = f32[512]{0:T(512)S(1)} all-reduce(f32[512]{0:T(512)S(1)} %get-tuple-element.129), channel_id=4, replica_groups=mesh['grp'=4,'mem'=8] {'mem'}, use_global_device_ids=true, to_apply=%region_17.18.clone | all-reduce | flops 512 | bytes 4096
  152.1 19.0 %reduce-scatter.6.cloned.1.call-done = f32[64,128]{1,0:T(8,128)} async-done(((f32[512,128]{1,0:T(8,128)}), f32[64,128]{1,0:T(8,128)}) %reduce-scatter.6.cloned.1.call-update) | async-done | bytes 32784 | tf_op jit(solution)/shard_map/reduce_scatter | solution.py:88
  171.1 19.9 %all-reduce.6 = (f32[64]{0:T(128)S(1)}, f32[64,128]{1,0:T(8,128)S(1)}) all-reduce(f32[64]{0:T(128)S(1)} %dynamic-slice.5, f32[64,128]{1,0:T(8,128)} %reduce-scatter.6.cloned.1.call-done), channel_id=1, replica_groups=mesh['grp'=4,'mem'=8] {'grp'}, use_global_device_ids=true, to_apply=%region_18.19 | all-reduce | flops 8256 | bytes 66048 | tf_op jit(solution)/shard_map/psum | solution.py:91
  191.2 9.3 %all_gather.22 = f32[512,64]{1,0:T(8,128)S(1)} all-gather(f32[64,64]{1,0:T(8,128)S(1)} %get-tuple-element.272), channel_id=1, replica_groups=mesh['grp'=4,'mem'=8] {'mem'}, dimensions={0}, use_global_device_ids=true | all-gather | bytes 147456 | tf_op jit(solution)/shard_map/all_gather | solution.py:97
  200.4 8.3 %all_gather.23 = f32[512,64]{1,0:T(8,128)S(1)} all-gather(f32[64,64]{1,0:T(8,128)S(1)} %get-tuple-element.273), channel_id=1, replica_groups=mesh['grp'=4,'mem'=8] {'mem'}, dimensions={0}, use_global_device_ids=true | all-gather | bytes 147456 | tf_op jit(solution)/shard_map/all_gather | solution.py:98
  208.8 13.4 %all-reduce.1 = f32[512]{0:T(512)S(1)} all-reduce(f32[512]{0:T(512)S(1)} %get-tuple-element.279), channel_id=1, replica_groups=mesh['grp'=4,'mem'=8] {'mem'}, use_global_device_ids=true, to_apply=%add.1 | all-reduce | flops 512 | bytes 4096
  222.5 12.2 %while.41 = (s32[]{:T(128)}, f32[512,128]{1,0:T(8,128)}, f32[512]{0:T(512)S(1)}, f32[512]{0:T(512)S(1)}, f32[2,1024,128]{2,1,0:T(8,128)S(1)}, /*index=5*/f32[512...) while((s32[]{:T(128)}, f32[512,128]{1,0:T(8,128)}, ...), condition=%wide.region_24.25_spmd.clone, body=%wide.region_20.24_spmd.clone.sunk | while | flops 1617559040 | bytes 10293372 | solution.py:40
  225.4 2.7 convolution_add_fusion.5
  231.1 3.7 %convolution_add_fusion.5 = f32[512,128]{1,0:T(8,128)} fusion(f32[2,1024,128]{2,1,0:T(8,128)S(1)} %get-tuple-element.505, s32[]{:T(128)} %get-tuple-element.491, f32[1024,512]{0,1:T(8,128)S(1)} %get-tuple-element.425, f32[1024]{0:T(1024)S(1)} %bitcast.55, f32[1024]{0:T(1024)S(1)} %fusion.65, f32[1024]{0:T(1024)S(1)} %get-tuple-element.426, ...), kind=kOutput, calls=%fused_computation.35.clone.1 | convolution fusion | flops 807010304 | bytes 3158021 | tf_op jit(solution)/shard_map/while/body/eval_jaxpr/dot_general | solution.py:26
  234.7 11.8 %all-reduce.4 = f32[512]{0:T(512)S(1)} all-reduce(f32[512]{0:T(512)S(1)} %get-tuple-element.132), channel_id=7, replica_groups=mesh['grp'=4,'mem'=8] {'mem'}, use_global_device_ids=true, to_apply=%region_27.28.clone | all-reduce | flops 512 | bytes 4096
  246.6 19.2 %reduce-scatter.8.cloned.1.call-done = f32[64,128]{1,0:T(8,128)} async-done(((f32[512,128]{1,0:T(8,128)}), f32[64,128]{1,0:T(8,128)}) %reduce-scatter.8.cloned.1.call-update) | async-done | bytes 32784 | tf_op jit(solution)/shard_map/reduce_scatter | solution.py:88
  265.8 19.9 %all-reduce.5 = (f32[64,128]{1,0:T(8,128)S(1)}, f32[64]{0:T(128)S(1)}) all-reduce(f32[64,128]{1,0:T(8,128)} %reduce-scatter.8.cloned.1.call-done, f32[64]{0:T(128)S(1)} %dynamic-slice.7), channel_id=1, replica_groups=mesh['grp'=4,'mem'=8] {'grp'}, use_global_device_ids=true, to_apply=%region_26.27 | all-reduce | flops 8256 | bytes 66048 | tf_op jit(solution)/shard_map/psum | solution.py:91
  (77 shorter events, 19.7 us)
Async XLA Ops:
  7.2 70.4 %reduce-scatter.4.cloned.1.call-start = ((), (), s32[]{:S(2)}) async-start(), calls=%async_computation.3 | async-start | bytes 294912 | tf_op jit(solution)/shard_map/reduce_scatter | solution.py:88
  8.5 1.5 copy-start.2
  8.5 1.5 copy-start.1
  10.1 51.9 %copy-start.3 = (u32[32]{0:T(128)S(1)}, u32[32]{0:T(128)}, u32[]{:S(2)}) copy-start(u32[32]{0:T(128)} %constant.58) | copy-start | bytes 388
  18.5 0.7 copy-start
  19.2 151.9 %reduce-scatter.6.cloned.1.call-start = ((), (), s32[]{:S(2)}) async-start(), calls=%async_computation.4 | async-start | bytes 294912 | tf_op jit(solution)/shard_map/reduce_scatter | solution.py:88
  140.1 125.7 %reduce-scatter.8.cloned.1.call-start = ((), (), s32[]{:S(2)}) async-start(), calls=%async_computation.5 | async-start | bytes 294912 | tf_op jit(solution)/shard_map/reduce_scatter | solution.py:88
Sparse Core Ops, SparseCore 0:
  19.3 36.3 reduce-scatter.3
  140.3 30.7 reduce-scatter.5
  234.9 30.9 reduce-scatter.7
where the time goes:
time: 294 us; the launch traced here: 293 us
  blocking collectives  199 us (68%)
  waiting for transfers between devices  38.3 us (13%)
  matrix products  28.4 us (10%)
  between operations  15.9 us (5%)
  other arithmetic  9.37 us (3%)
    unnamed x5, blocking collectives  63.3 us
    psum x3, blocking collectives, combine(): return lax.psum((shared[0], shared[1]), 'grp')  58.5 us
    psum x1, blocking collectives, shards(): total = lax.psum(jnp.sum(virtual), ('grp', 'mem'))  42.2 us
    reduce_scatter x3, waiting for transfers between devices, combine(): lax.psum_scatter(local_sums, 'mem', scatter_dimension=0, tiled=True)  38.2 us
    dot_general x6, matrix products, advance(): lax.dot_general(weights, piece[0], (((0,), (0,)), ((), ())), precision=la...  20.3 us
    all_gather x2, blocking collectives, shards(): lax.all_gather(means, 'mem', axis=0, tiled=True)  18.4 us
    all_gather x2, blocking collectives, shards(): lax.all_gather(variances, 'mem', axis=0, tiled=True)  16.8 us
    dot_general x4, matrix products, soft_weights(): lax.dot_general(block_features, table, (((1,), (1,)), ((), ())), precisio...  8.14 us
  transfers between devices with their start and end apart: 3, of which 2 were waited for; matrix products, arithmetic and copies ran while one was open for 0% of the time, Pallas kernels for 0%

commit v1 on v0

v1 whole, which is shorter than its diff:
```python
import functools
import math

import jax
import jax.numpy as jnp
from jax import lax
from jax.experimental import pallas as pl
from jax.experimental.pallas import tpu as pltpu
from jax.sharding import PartitionSpec as P

P_SIZE = 512
ITERS = 2
LANES = 128
SUB = 8
CHUNK = 512
F32 = jnp.float32
BF16 = jnp.bfloat16
MESH = pl.DeviceIdType.MESH


def split3(value):
    first = value.astype(BF16)
    rest = value - first.astype(F32)
    second = rest.astype(BF16)
    third = (rest - second.astype(F32)).astype(BF16)
    return first, second, third


def dot(left, right):
    return lax.dot_general(left, right, (((1,), (0,)), ((), ())), preferred_element_type=F32)


def kernel(n_mem, n_grp, means_ref, variances_ref, virtual_ref, assign_ref,
           out_means_ref, out_variances_ref, out_weights_ref,
           wide, tall, acc, cnt, shares, landed, groups, tables, virt,
           rs_send, rs_recv, z_send, z_recv, ag_send, ag_recv):
    mem, grp = lax.axis_index("mem"), lax.axis_index("grp")
    width, children = means_ref.shape
    feats = 2 * width
    rows = P_SIZE // n_mem
    turns = children // CHUNK

    def member(step):
        return lax.rem(mem + step, n_mem)

    def group(step):
        return lax.rem(grp + step, n_grp)

    barrier = pltpu.get_barrier_semaphore()
    for step in range(1, n_mem):
        pl.semaphore_signal(barrier, inc=1, device_id={"mem": member(step)}, device_id_type=MESH)
    for step in range(1, n_grp):
        pl.semaphore_signal(barrier, inc=1, device_id={"grp": group(step)}, device_id_type=MESH)

    virt[...] = virtual_ref[...].astype(F32)
    lane = lax.broadcasted_iota(jnp.int32, (rows, LANES), 1)
    diagonal = lane == lax.broadcasted_iota(jnp.int32, (rows, LANES), 0)
    low = lane < width

    def as_row(column):
        return jnp.sum(jnp.where(diagonal, column, 0.0), axis=0, keepdims=True)

    def as_column(row):
        return jnp.sum(jnp.where(diagonal, row, 0.0), axis=1, keepdims=True)

    def fold(weights):
        total = weights[:, :LANES]
        for at in range(LANES, CHUNK, LANES):
            total = total + weights[:, at:at + LANES]
        return total

    def add(turn, sums, counts):
        if turn == 0:
            acc[...] = sums
            cnt[...] = counts
        else:
            acc[...] += sums
            cnt[...] += counts

    def initial(turn):
        span = slice(turn * CHUNK, (turn + 1) * CHUNK)
        mean = means_ref[:, span]
        feature = jnp.concatenate([mean, variances_ref[:, span] + mean * mean], axis=0)
        one, two, three = split3(feature)
        for at, part in enumerate((one, two, three, one, two, one)):
            wide[at * feats:(at + 1) * feats, span] = part
        one, two, three = split3(feature.T)
        for at, part in enumerate((one, two, three)):
            tall[span, at * feats:(at + 1) * feats] = part
        label = lax.broadcasted_iota(jnp.int32, (P_SIZE, CHUNK), 0)
        weights = jnp.where(label == assign_ref[:, span], virt[:, span], 0.0)
        parts = dot(weights.astype(BF16), tall[span, :])
        sums = parts[:, 2 * feats:] + parts[:, feats:2 * feats] + parts[:, :feats]
        add(turn, sums, fold(weights))

    def soft(turn, table, offset, log_weight):
        span = slice(turn * CHUNK, (turn + 1) * CHUNK)
        virtual = virt[:, span]
        score = log_weight + virtual * (dot(table, wide[:, span]) + offset)
        top = jnp.max(score, axis=0, keepdims=True)
        expd = jnp.exp(score - top)
        weights = expd * (virtual / jnp.sum(expd, axis=0, keepdims=True))
        first = weights.astype(BF16)
        second = (weights - first.astype(F32)).astype(BF16)
        high = dot(first, tall[span, :])
        small = dot(second, tall[span, :2 * feats])
        sums = (high[:, 2 * feats:] + small[:, feats:]) + (high[:, feats:2 * feats] + small[:, :feats])
        add(turn, sums + high[:, :feats], fold(weights))

    def combine(turn, local_total):
        counts = jnp.sum(cnt[...], axis=1, keepdims=True)
        for at in range(n_mem):
            span = slice(at * rows, (at + 1) * rows)
            shares[turn, at, :rows, :] = acc[span, :]
            row = as_row(counts[span, :])
            if local_total is not None:
                row = jnp.where(lane[:1, :] == LANES - 1, local_total, row)
            shares[turn, at, rows:, :] = jnp.broadcast_to(row, (SUB, LANES))
        if turn == 0:
            pl.semaphore_wait(barrier, n_mem + n_grp - 2)
        copies = [pltpu.make_async_remote_copy(
            src_ref=shares.at[turn, member(step)], dst_ref=landed.at[turn, step],
            send_sem=rs_send.at[turn, step], recv_sem=rs_recv.at[turn, step],
            device_id={"mem": member(step)}, device_id_type=MESH) for step in range(1, n_mem)]
        for copy in copies:
            copy.start()
        total = shares[turn, mem]
        for step, copy in enumerate(copies, 1):
            copy.wait_recv()
            total = total + landed[turn, step]
        groups[turn, grp] = total
        crossing = [pltpu.make_async_remote_copy(
            src_ref=groups.at[turn, grp], dst_ref=groups.at[turn, grp],
            send_sem=z_send.at[turn, step], recv_sem=z_recv.at[turn, step],
            device_id={"grp": group(step)}, device_id_type=MESH) for step in range(1, n_grp)]
        for copy in crossing:
            copy.start()
        for copy in crossing:
            copy.wait_recv()
        total = groups[turn, 0]
        for at in range(1, n_grp):
            total = total + groups[turn, at]
        return total, copies + crossing

    def maximize(total):
        mass = as_column(total[rows:rows + 1, :]) + 1.0
        scaled = (total[:rows, :] + jnp.where(low, 0.0, 1.0)) / mass
        turned = pltpu.roll(scaled, width, 1)
        means = jnp.where(low, scaled, turned)
        variances = jnp.where(low, turned, scaled) - means * means
        return mass, means, variances

    def spread(turn, mass, means, variances, everything):
        inverse = 1.0 / variances
        scale = -0.5 / width
        terms = jnp.log(2.0 * math.pi * variances) + means * means * inverse
        offset = scale * jnp.sum(jnp.where(low, terms, 0.0), axis=1, keepdims=True)
        log_weight = jnp.log(mass / (everything + P_SIZE))
        tables[turn, mem, :rows, :] = scale * jnp.where(low, -2.0 * means * inverse, inverse)
        tail = lax.broadcasted_iota(jnp.int32, (SUB, LANES), 0) == 0
        tables[turn, mem, rows:, :] = jnp.where(tail, as_row(offset), as_row(log_weight))
        copies = [pltpu.make_async_remote_copy(
            src_ref=tables.at[turn, mem], dst_ref=tables.at[turn, mem],
            send_sem=ag_send.at[turn, step], recv_sem=ag_recv.at[turn, step],
            device_id={"mem": member(step)}, device_id_type=MESH) for step in range(1, n_mem)]
        for copy in copies:
            copy.start()
        for copy in copies:
            copy.wait_recv()
        return copies

    def gathered(turn):
        table = jnp.concatenate([tables[turn, at, :rows, :] for at in range(n_mem)], axis=0)
        offset = jnp.concatenate([as_column(tables[turn, at, rows:rows + 1, :]) for at in range(n_mem)], axis=0)
        log_weight = jnp.concatenate([as_column(tables[turn, at, rows + 1:rows + 2, :]) for at in range(n_mem)], axis=0)
        one, two, three = split3(table)
        return jnp.concatenate([one, one, one, two, two, three], axis=1), offset, log_weight

    for turn in range(turns):
        initial(turn)
    total, sent = combine(0, jnp.sum(virt[...], axis=1, keepdims=True))
    everything = total[rows:rows + 1, LANES - 1:]
    mass, means, variances = maximize(total)
    for iteration in range(ITERS):
        sent += spread(iteration, mass, means, variances, everything)
        parameters = gathered(iteration)
        for turn in range(turns):
            soft(turn, *parameters)
        total, more = combine(iteration + 1, None)
        sent += more
        mass, means, variances = maximize(total)
    out_means_ref[...] = means[:, :width]
    out_variances_ref[...] = variances[:, :width]
    out_weights_ref[...] = as_row(mass / (everything + P_SIZE))[:, :rows]
    for copy in sent:
        copy.wait_send()


def solution(mesh):
    n_grp, n_mem = mesh.shape["grp"], mesh.shape["mem"]
    rows = P_SIZE // n_mem

    def shards(child_means, child_variances, virtual_counts, assignment):
        children, width = child_means.shape
        feats = 2 * width
        rounds = ITERS + 1
        whole = pl.BlockSpec(memory_space=pltpu.VMEM)
        means, variances, weights = pl.pallas_call(
            functools.partial(kernel, n_mem, n_grp),
            out_shape=(
                jax.ShapeDtypeStruct((rows, width), F32),
                jax.ShapeDtypeStruct((rows, width), F32),
                jax.ShapeDtypeStruct((1, rows), F32),
            ),
            in_specs=[whole] * 4,
            out_specs=(whole,) * 3,
            scratch_shapes=[
                pltpu.VMEM((6 * feats, children), BF16),
                pltpu.VMEM((children, 3 * feats), BF16),
                pltpu.VMEM((P_SIZE, feats), F32),
                pltpu.VMEM((P_SIZE, LANES), F32),
                pltpu.VMEM((rounds, n_mem, rows + SUB, LANES), F32),
                pltpu.VMEM((rounds, n_mem, rows + SUB, LANES), F32),
                pltpu.VMEM((rounds, n_grp, rows + SUB, LANES), F32),
                pltpu.VMEM((ITERS, n_mem, rows + SUB, LANES), F32),
                pltpu.VMEM((1, children), F32),
                pltpu.SemaphoreType.DMA((rounds, n_mem)),
                pltpu.SemaphoreType.DMA((rounds, n_mem)),
                pltpu.SemaphoreType.DMA((rounds, n_grp)),
                pltpu.SemaphoreType.DMA((rounds, n_grp)),
                pltpu.SemaphoreType.DMA((ITERS, n_mem)),
                pltpu.SemaphoreType.DMA((ITERS, n_mem)),
            ],
            compiler_params=pltpu.CompilerParams(collective_id=0, has_side_effects=True),
        )(child_means.T, child_variances.T, virtual_counts.reshape(1, children), assignment.T)
        return means, variances, weights.reshape(rows)

    in_specs = (
        P(("grp", "mem"), None),
        P(("grp", "mem"), None),
        P(("grp", "mem")),
        P(("grp", "mem"), None),
    )
    out_specs = (P("mem", None), P("mem", None), P("mem"))
    return jax.shard_map(shards, mesh=mesh, in_specs=in_specs, out_specs=out_specs, check_vma=False)
```

time: 294 us -> 62.2 us (0.21)
  blocking collectives: 199 us -> 0 us
  Pallas kernels: 0 us -> 58.8 us
  waiting for transfers between devices: 38.3 us -> 0 us
  matrix products: 28.4 us -> 0 us
  between operations: 15.9 us -> 0.65 us
  other arithmetic: 9.37 us -> 0 us
    psum x4 -> x0, blocking collectives: 101 us -> none  [the longest x3 58.5 us: combine(): return lax.psum((shared[0], shared[1]), 'grp')]
    unnamed x5 -> x0, blocking collectives: 63.3 us -> none
    pallas_call x0 -> x1, Pallas kernels: none -> 58.8 us  [shards(): pl.pallas_call(functools.partial(kernel, n_mem, n_grp), out_shape=(jax.Sh...]
    reduce_scatter x3 -> x0, waiting for transfers between devices: 38.2 us -> none  [combine(): lax.psum_scatter(local_sums, 'mem', scatter_dimension=0, tiled=True)]
    all_gather x4 -> x0, blocking collectives: 35.2 us -> none  [the longest x2 18.4 us: shards(): lax.all_gather(means, 'mem', axis=0, tiled=True)]
    dot_general x10 -> x0, matrix products: 28.4 us -> none  [the longest x6 20.3 us: advance(): lax.dot_general(weights, piece[0], (((0,), (0,)), ((), ())), precision=la...]
    reduce_sum x13 -> x0, other arithmetic: 4.97 us -> none  [the longest x6 2.68 us: advance(): counts = carry[1] + jnp.sum(weights, axis=0)]
  transfers between devices with their start and end apart: 3 -> 0, of which waited for: 2 -> 0; matrix products, arithmetic and copies ran while one was open for 0% -> 0% of each run, Pallas kernels for 0% -> 0%
where the time goes in v1:
time: 62.2 us; the launch traced here: 62 us
  Pallas kernels  58.8 us (95%)
  local copies, waits for them, and re-layouts  2.57 us (4%)
  between operations  0.65 us (1%)
    pallas_call x1, Pallas kernels, shards(): pl.pallas_call(functools.partial(kernel, n_mem, n_grp), out_shape=(jax.Sh...  58.8 us
    unnamed x7, local copies, waits for them, and re-layouts  2.57 us

profile of v1, /device:TPU:0, one launch (start us, length us, event | category | flops | bytes accessed | tf_op | source)
XLA Modules:
  0.0 62.0 jit_solution(10315096101323090350)
XLA Ops:
  0.6 58.8 %shard_map.67 = (f32[64,64]{1,0:T(8,128)}, f32[64,64]{1,0:T(8,128)}, f32[1,64]{1,0:T(1,128)}) custom-call(f32[64,2048]{1,0:T(8,128)} %bitcast.5, f32[64,2048]{1,0:T(8,128)} %bitcast.6, s32[1,2048]{1,0:T(1,128)} %bitcast.7, s32[1,2048]{1,0:T(1,128)} %bitcast.8), custom_call_target="tpu_custom_call" | custom-call | tf_op jit(solution)/shard_map/pallas_call | solution.py:208
  59.4 0.0 copy-start
  59.4 1.4 %copy.10 = f32[64,64]{1,0:T(8,128)} copy(f32[64,64]{1,0:T(8,128)} %get-tuple-element.12) | data formatting | bytes 32768
  60.8 0.0 copy-done
  60.8 0.0 copy-start.1
  60.8 0.6 copy.11
  61.4 0.1 copy-done.1
  61.5 0.5 copy.12
Async XLA Ops:
  59.4 1.4 %copy-start = (f32[64,64]{1,0:T(8,128)S(1)}, f32[64,64]{1,0:T(8,128)}, u32[]{:S(2)}) copy-start(f32[64,64]{1,0:T(8,128)} %get-tuple-element.13) | copy-start | bytes 49156
  60.8 0.7 %copy-start.1 = (f32[1,64]{1,0:T(1,128)S(1)}, f32[1,64]{1,0:T(1,128)}, u32[]{:S(2)}) copy-start(f32[1,64]{1,0:T(1,128)} %get-tuple-element.8) | copy-start | bytes 772

commit v2 on v1

v2 whole, which is shorter than its diff:
```python
import functools
import math

import jax
import jax.numpy as jnp
from jax import lax
from jax.experimental import pallas as pl
from jax.experimental.pallas import tpu as pltpu
from jax.sharding import PartitionSpec as P

P_SIZE = 512
ITERS = 2
LANES = 128
SUB = 8
CHUNK = 512
PARTS = 2
LOG2E = 1.0 / math.log(2.0)
F32 = jnp.float32
BF16 = jnp.bfloat16
MESH = pl.DeviceIdType.MESH


def split3(value):
    first = value.astype(BF16)
    rest = value - first.astype(F32)
    second = rest.astype(BF16)
    third = (rest - second.astype(F32)).astype(BF16)
    return first, second, third


def dot(left, right):
    return lax.dot_general(left, right, (((1,), (0,)), ((), ())), preferred_element_type=F32)


def kernel(n_mem, n_grp, means_hbm, variances_hbm, virtual_hbm, assign_hbm, packed_ref,
           means_ref, variances_ref, virtual_ref, assign_ref, in_sem,
           wide, tall, scores, first, second, shares, landed, groups, tables, virt,
           rs_send, rs_recv, z_send, z_recv, ag_send, ag_recv):
    mem, grp = lax.axis_index("mem"), lax.axis_index("grp")
    width, children = means_ref.shape
    feats = 2 * width
    rows = P_SIZE // n_mem
    part = rows // PARTS
    block = P_SIZE // PARTS
    turns = children // CHUNK
    mem_steps = tuple(reversed(range(1, n_mem)))
    grp_steps = sorted(range(1, n_grp), key=lambda at: -min(at, n_grp - at))

    def member(step):
        peer, bit = mem, 1
        while bit < n_mem:
            if step & bit:
                peer = peer + bit * (1 - 2 * lax.rem(mem // bit, 2))
            bit *= 2
        return peer

    def group(step):
        return lax.rem(grp + step, n_grp)

    barrier = pltpu.get_barrier_semaphore()
    for step in range(1, n_mem):
        pl.semaphore_signal(barrier, inc=1, device_id={"mem": member(step)}, device_id_type=MESH)
    for step in range(1, n_grp):
        pl.semaphore_signal(barrier, inc=1, device_id={"grp": group(step)}, device_id_type=MESH)

    loads = [pltpu.make_async_copy(source, target, in_sem.at[at]) for at, (source, target) in enumerate((
        (virtual_hbm, virtual_ref), (assign_hbm, assign_ref), (means_hbm, means_ref), (variances_hbm, variances_ref)))]
    for load in loads:
        load.start()
    for load in loads:
        load.wait()
    virt[...] = virtual_ref[...].astype(F32)
    tall[:, 3 * feats:] = jnp.ones((children, LANES), BF16)
    lane = lax.broadcasted_iota(jnp.int32, (part, LANES), 1)
    line = lax.broadcasted_iota(jnp.int32, (part, LANES), 0)
    low = lane < width

    def as_row(column, piece=0):
        return jnp.sum(jnp.where(lane == line + piece * part, column, 0.0), axis=0, keepdims=True)

    def as_column(row):
        return jnp.sum(jnp.where(lane == line, row, 0.0), axis=1, keepdims=True)

    def remote(source, target, send, recv, device):
        return pltpu.make_async_remote_copy(
            src_ref=source, dst_ref=target, send_sem=send, recv_sem=recv, device_id=device, device_id_type=MESH)

    def initial(turn):
        span = slice(turn * CHUNK, (turn + 1) * CHUNK)
        mean = means_ref[:, span]
        feature = jnp.concatenate([mean, variances_ref[:, span] + mean * mean], axis=0)
        one, two, three = split3(feature)
        for at, value in enumerate((one, two, three, one, two, one)):
            wide[at * feats:(at + 1) * feats, span] = value
        one, two, three = split3(feature.T)
        for at, value in enumerate((three, two, one)):
            tall[span, at * feats:(at + 1) * feats] = value
        place = lax.broadcasted_iota(jnp.int32, (P_SIZE, 1), 0)
        owner = lax.rem(place, block)
        label = (owner // part) * rows + (place // block) * part + lax.rem(owner, part)
        weights = jnp.where(label == assign_ref[:, span], virt[:, span], 0.0)
        first[:, span] = weights.astype(BF16)

    def soft(turn):
        span = slice(turn * CHUNK, (turn + 1) * CHUNK)
        score = scores[:, span]
        expd = jnp.exp2(score - jnp.max(score, axis=0, keepdims=True))
        weights = expd * (virt[:, span] / jnp.sum(expd, axis=0, keepdims=True))
        high = weights.astype(BF16)
        first[:, span] = high
        second[:, span] = (weights - high.astype(F32)).astype(BF16)

    def statistics(turn, piece):
        span = slice(piece * block, (piece + 1) * block)
        high = dot(first[span, :], tall[...])
        sums, main, counts = high[:, :feats] + high[:, feats:2 * feats], high[:, 2 * feats:3 * feats], high[:, 3 * feats:]
        if turn > 0:
            small = dot(second[span, :], tall[:, 2 * feats:])
            sums, counts = sums + small[:, :feats], counts + small[:, feats:]
        return sums + main, counts

    def combine(turn, local_total):
        sent, scattered, crossing = [], [], []
        for piece in range(PARTS):
            sums, counts = statistics(turn, piece)
            for at in range(n_mem):
                span = slice(at * part, (at + 1) * part)
                row = as_row(counts[span, :])
                if local_total is not None:
                    row = jnp.where(lane[:1, :] == LANES - 1, local_total, row)
                shares[turn, piece, at, :part, :] = sums[span, :]
                shares[turn, piece, at, part:part + 1, :] = row
            if turn == 0 and piece == 0:
                pl.semaphore_wait(barrier, n_mem + n_grp - 2)
            span = pl.ds(0, part + 1)
            scattered.append([remote(
                shares.at[turn, piece, member(step), span], landed.at[turn, piece, step, span],
                rs_send.at[turn, piece, step], rs_recv.at[turn, piece, step],
                {"mem": member(step)}) for step in mem_steps])
            for copy in scattered[-1]:
                copy.start()
            sent += scattered[-1]
        for piece in range(PARTS):
            total = shares[turn, piece, mem, :part + 1]
            for step, copy in zip(mem_steps, scattered[piece]):
                copy.wait_recv()
                total = total + landed[turn, piece, step, :part + 1]
            groups[turn, piece, grp, :part + 1] = total
            crossing.append([remote(
                groups.at[turn, piece, grp, span], groups.at[turn, piece, grp, span],
                z_send.at[turn, piece, step], z_recv.at[turn, piece, step],
                {"grp": group(step)}) for step in grp_steps])
            for copy in crossing[-1]:
                copy.start()
            sent += crossing[-1]
        return sent, crossing

    def received(turn, piece, crossing):
        for copy in crossing[piece]:
            copy.wait_recv()
        total = groups[turn, piece, 0, :part + 1]
        for at in range(1, n_grp):
            total = total + groups[turn, piece, at, :part + 1]
        return total

    def maximize(total):
        mass = as_column(total[part:part + 1, :]) + 1.0
        scaled = (total[:part, :] + jnp.where(low, 0.0, 1.0)) / mass
        turned = pltpu.roll(scaled, width, 1)
        means = jnp.where(low, scaled, turned)
        variances = jnp.where(low, turned, scaled) - means * means
        return mass, means, variances

    def spread(turn, piece, mass, means, variances, everything):
        inverse = 1.0 / variances
        scale = -0.5 / width * LOG2E
        terms = jnp.log(2.0 * math.pi * variances) + means * means * inverse
        offset = scale * jnp.sum(jnp.where(low, terms, 0.0), axis=1, keepdims=True)
        log_weight = LOG2E * jnp.log(mass / (everything + P_SIZE))
        tables[turn, piece, mem, :part, :] = scale * jnp.where(low, -2.0 * means * inverse, inverse)
        tables[turn, piece, mem, part:part + 1, :] = as_row(offset)
        tables[turn, piece, mem, part + 1:part + 2, :] = as_row(log_weight)
        span = pl.ds(0, part + 2)
        copies = [remote(
            tables.at[turn, piece, mem, span], tables.at[turn, piece, mem, span],
            ag_send.at[turn, piece, step], ag_recv.at[turn, piece, step],
            {"mem": member(step)}) for step in mem_steps]
        for copy in copies:
            copy.start()
        return copies

    def score(turn, piece):
        held = tables.at[turn, piece]
        table = jnp.concatenate([held[at, :part, :] for at in range(n_mem)], axis=0)
        offset = jnp.concatenate([as_column(held[at, part:part + 1, :]) for at in range(n_mem)], axis=0)
        log_weight = jnp.concatenate([as_column(held[at, part + 1:part + 2, :]) for at in range(n_mem)], axis=0)
        one, two, three = split3(table)
        table = jnp.concatenate([one, one, one, two, two, three], axis=1)
        for turn in range(turns):
            span = slice(turn * CHUNK, (turn + 1) * CHUNK)
            scores[piece * block:(piece + 1) * block, span] = (
                log_weight + virt[:, span] * (dot(table, wide[:, span]) + offset))

    for turn in range(turns):
        initial(turn)
    sent, crossing = combine(0, jnp.sum(virt[...], axis=1, keepdims=True))
    everything = None
    for iteration in range(ITERS):
        gathers = []
        for piece in range(PARTS):
            total = received(iteration, piece, crossing)
            if everything is None:
                everything = total[part:part + 1, LANES - 1:]
            gathers.append(spread(iteration, piece, *maximize(total), everything))
        for piece in range(PARTS):
            for copy in gathers[piece]:
                copy.wait_recv()
            score(iteration, piece)
            sent += gathers[piece]
        for turn in range(turns):
            soft(turn)
        more, crossing = combine(iteration + 1, None)
        sent += more
    shown = jnp.zeros((1, LANES), F32)
    for piece in range(PARTS):
        total = received(ITERS, piece, crossing)
        mass, means, variances = maximize(total)
        packed_ref[piece * part:(piece + 1) * part, :] = jnp.where(low, means, variances)
        shown = shown + as_row(mass / (everything + P_SIZE), piece)
    packed_ref[rows:, :] = jnp.broadcast_to(shown, (SUB, LANES))
    for copy in sent:
        copy.wait_send()


def unpack(packed_ref, means_ref, variances_ref, weights_ref):
    rows, width = means_ref.shape
    packed = packed_ref[:rows, :]
    means_ref[...] = packed[:, :width]
    variances_ref[...] = pltpu.roll(packed, width, 1)[:, :width]
    weights_ref[...] = packed_ref[rows:rows + 1, :rows]


def solution(mesh):
    n_grp, n_mem = mesh.shape["grp"], mesh.shape["mem"]
    rows = P_SIZE // n_mem

    def shards(child_means, child_variances, virtual_counts, assignment):
        children, width = child_means.shape
        feats = 2 * width
        rounds = ITERS + 1
        whole = pl.BlockSpec(memory_space=pltpu.VMEM)
        part = rows // PARTS
        packed = pl.pallas_call(
            functools.partial(kernel, n_mem, n_grp),
            out_shape=jax.ShapeDtypeStruct((rows + SUB, LANES), F32),
            in_specs=[pl.BlockSpec(memory_space=pl.ANY)] * 4,
            out_specs=whole,
            scratch_shapes=[
                pltpu.VMEM((width, children), F32),
                pltpu.VMEM((width, children), F32),
                pltpu.VMEM((1, children), jnp.int32),
                pltpu.VMEM((1, children), jnp.int32),
                pltpu.SemaphoreType.DMA((4,)),
                pltpu.VMEM((6 * feats, children), BF16),
                pltpu.VMEM((children, 3 * feats + LANES), BF16),
                pltpu.VMEM((P_SIZE, children), F32),
                pltpu.VMEM((P_SIZE, children), BF16),
                pltpu.VMEM((P_SIZE, children), BF16),
                pltpu.VMEM((rounds, PARTS, n_mem, part + SUB, LANES), F32),
                pltpu.VMEM((rounds, PARTS, n_mem, part + SUB, LANES), F32),
                pltpu.VMEM((rounds, PARTS, n_grp, part + SUB, LANES), F32),
                pltpu.VMEM((ITERS, PARTS, n_mem, part + SUB, LANES), F32),
                pltpu.VMEM((1, children), F32),
                pltpu.SemaphoreType.DMA((rounds, PARTS, n_mem)),
                pltpu.SemaphoreType.DMA((rounds, PARTS, n_mem)),
                pltpu.SemaphoreType.DMA((rounds, PARTS, n_grp)),
                pltpu.SemaphoreType.DMA((rounds, PARTS, n_grp)),
                pltpu.SemaphoreType.DMA((ITERS, PARTS, n_mem)),
                pltpu.SemaphoreType.DMA((ITERS, PARTS, n_mem)),
            ],
            compiler_params=pltpu.CompilerParams(collective_id=0, has_side_effects=True),
        )(child_means.T, child_variances.T, virtual_counts.reshape(1, children), assignment.T)
        means, variances, weights = pl.pallas_call(
            unpack,
            out_shape=(
                jax.ShapeDtypeStruct((rows, width), F32),
                jax.ShapeDtypeStruct((rows, width), F32),
                jax.ShapeDtypeStruct((1, rows), F32),
            ),
            in_specs=[whole],
            out_specs=(whole,) * 3,
        )(packed)
        return means, variances, weights.reshape(rows)

    in_specs = (
        P(("grp", "mem"), None),
        P(("grp", "mem"), None),
        P(("grp", "mem")),
        P(("grp", "mem"), None),
    )
    out_specs = (P("mem", None), P("mem", None), P("mem"))
    return jax.shard_map(shards, mesh=mesh, in_specs=in_specs, out_specs=out_specs, check_vma=False)
```

time: 62.2 us -> 51.5 us (0.83)
  Pallas kernels: 58.8 us -> 50.7 us
  local copies, waits for them, and re-layouts: 2.57 us -> 0 us
    pallas_call x1 -> x2, Pallas kernels: 58.8 us -> 50.7 us  [the longest x1 49.2 us: shards(): pl.pallas_call(functools.partial(kernel, n_mem, n_grp), out_shape=jax.Sha...]
    unnamed x7 -> x0, local copies, waits for them, and re-layouts: 2.57 us -> none
where the time goes in v2:
time: 51.5 us; the launch traced here: 51.3 us
  Pallas kernels  50.7 us (98%)
  between operations  0.64 us (1%)
    pallas_call x1, Pallas kernels, shards(): pl.pallas_call(functools.partial(kernel, n_mem, n_grp), out_shape=jax.Sha...  49.2 us
    pallas_call x1, Pallas kernels, shards(): pl.pallas_call(unpack, out_shape=(jax.ShapeDtypeStruct((rows, width), F32...  1.46 us

profile of v2, /device:TPU:0, one launch (start us, length us, event | category | flops | bytes accessed | tf_op | source)
XLA Modules:
  0.0 51.3 jit_solution(8698839556509503020)
XLA Ops:
  0.6 49.2 %shard_map.67.packed_ref = f32[72,128]{1,0:T(8,128)} custom-call(f32[64,2048]{1,0:T(8,128)} %bitcast.5, f32[64,2048]{1,0:T(8,128)} %bitcast.6, s32[1,2048]{1,0:T(1,128)} %bitcast.7, s32[1,2048]{1,0:T(1,128)} %bitcast.8), custom_call_target="tpu_custom_call" | custom-call | tf_op jit(solution)/shard_map/pallas_call | solution.py:253
  49.9 1.5 %shard_map.68 = (f32[64,64]{1,0:T(8,128)}, f32[64,64]{1,0:T(8,128)}, f32[1,64]{1,0:T(1,128)}) custom-call(f32[72,128]{1,0:T(8,128)} %shard_map.67.packed_ref), custom_call_target="tpu_custom_call" | custom-call | tf_op jit(solution)/shard_map/pallas_call | solution.py:283
